TPU v7x, 256 devices: a whole 4x4x8 slice. The times are simulated.
256 devices in a mesh: section: 8 (over x, core), dp: 32 (over y, z).
Axes of the slice: x: 4, y: 4, z: 8, core: 2. Of those that a mesh axis runs over, the one named last changes fastest.
Arguments:
- inputs: bfloat16 [2, 4096, 1536], P(None, 'dp'), may hold values from -6 to 6
- grad_out: bfloat16 [2, 4096, 1536], P(None, 'dp'), may hold values from -6 to 6
- w_conv: bfloat16 [8, 4608, 768], P('section'), may hold values from -0.09375 to 0.09375
- w_point: bfloat16 [8, 768, 1536], P('section'), may hold values from -0.21875 to 0.21875
- gain_conv: float32 [8, 1536], P('section'), may hold values from 0.25 to 1.75
- gain_point: float32 [8, 768], P('section'), may hold values from 0.25 to 1.75
Outputs:
- grad_w_conv: float32 [8, 4608, 768], P('section', 'dp')
- grad_w_point: float32 [8, 768, 1536], P('section', 'dp')
- grad_gain_conv: float32 [8, 1536], P('section', 'dp')
- grad_gain_point: float32 [8, 768], P('section', 'dp')
- grad_acts: bfloat16 [8, 2, 4096, 1536], P('section', None, 'dp')
All inputs are finite; a program needn't handle non-finite values.
Results may differ from a plain program's by a relative error of at most 0.034.
Values may be sent and summed in bfloat16 or wider, within the bound.
No kernel may reach another device: no remote copies, remote signals or barrier semaphores. Data moves between devices by JAX's collectives and lax.ppermute only.
A program may use at most 128 MiB of HBM per device.

v0:
```python
import math

import jax
import jax.numpy as jnp
from jax import lax
from jax.sharding import PartitionSpec as P

EPSILON = 1e-06


def with_halo(cells, sides, width):
    for axis, dim in sides:
        count = lax.axis_size(axis)
        ends = count - 1
        head = lax.slice_in_dim(cells, 0, width, axis=dim)
        tail = lax.slice_in_dim(cells, cells.shape[dim] - width, cells.shape[dim], axis=dim)
        cells = jnp.concatenate(
            [
                lax.ppermute(tail, axis, [(i, (i + 1) % count) for i in range(ends)]),
                cells,
                lax.ppermute(head, axis, [((i + 1) % count, i) for i in range(ends)]),
            ],
            axis=dim,
        )
    return cells


def shifted(shard, axis, by):
    devices = lax.axis_size(axis)
    pairs = [(i, i + by) for i in range(devices) if 0 <= i + by < devices]
    return lax.ppermute(shard, axis, pairs)


def norm_act(values, scales):
    mean_sq = jnp.mean(values * values, axis=-1, keepdims=True)
    return jax.nn.gelu(values * lax.rsqrt(mean_sq + EPSILON) * scales)


def tap_columns(padded, dilation, reach, positions):
    earlier = lax.dynamic_slice_in_dim(padded, reach - dilation, positions, 0)
    central = lax.dynamic_slice_in_dim(padded, reach, positions, 0)
    later_rows = lax.dynamic_slice_in_dim(padded, reach + dilation, positions, 0)
    return jnp.concatenate([earlier, central, later_rows], axis=-1)


def contract_rows(left, right):
    return lax.dot_general(
        left, right, (((0,), (0,)), ((), ())), preferred_element_type=jnp.float32
    )


def times_transposed(left, right):
    return lax.dot_general(
        left, right, (((1,), (1,)), ((), ())), preferred_element_type=jnp.float32
    )


def on_device(inputs, grad_out, w_conv, w_point, gain_conv, gain_point):
    micro_count, positions, channels = inputs.shape
    section_index = lax.axis_index("section")
    section_count = lax.axis_size("section")
    group_size = lax.axis_size("dp")
    norm_scale = 1.0 / math.sqrt(micro_count * positions * group_size)
    reach = 3 ** (section_count - 1) // 2 ** (section_count - 1)
    dilation_table = jnp.array(
        [3**depth_index // 2**depth_index for depth_index in range(section_count)], jnp.int32
    )
    dilation = dilation_table[section_index]
    weight_conv = w_conv[0]
    weight_point = w_point[0]
    scale_conv = gain_conv[0]
    scale_point = gain_point[0]
    inner = weight_conv.shape[1]
    tap_weights = weight_conv.reshape(3, channels, inner)
    tick_total = section_count + micro_count - 1
    all_ticks = jnp.arange(tick_total, dtype=jnp.int32)
    zero_rows = jnp.zeros((positions, channels), jnp.bfloat16)

    def forward_tick(state_tuple, tick_index):
        received, stored, padded_store, kept_conv = state_tuple
        micro_step = tick_index - section_index
        active = (micro_step >= 0) & (micro_step < micro_count)
        slot_index = jnp.clip(micro_step, 0, micro_count - 1)
        own_rows = lax.dynamic_index_in_dim(inputs, slot_index, 0, keepdims=False)
        incoming = jnp.where(section_index == 0, own_rows, received)
        widened = incoming.astype(jnp.float32)
        activations = norm_act(widened, scale_conv).astype(jnp.bfloat16)
        padded = with_halo(activations, (("dp", 0),), reach)

        def compute():
            columns = tap_columns(padded, dilation, reach, positions)
            conv_out = jnp.dot(columns, weight_conv, preferred_element_type=jnp.float32)
            mixture = norm_act(conv_out, scale_point).astype(jnp.bfloat16)
            branch = jnp.dot(mixture, weight_point, preferred_element_type=jnp.float32)
            return ((widened + branch).astype(jnp.bfloat16), conv_out)

        def nothing():
            return (zero_rows, jnp.zeros((positions, inner), jnp.float32))

        outputs, conv_out = lax.cond(active, compute, nothing)
        stored = jnp.where(
            active, lax.dynamic_update_index_in_dim(stored, incoming, slot_index, 0), stored
        )
        padded_store = jnp.where(
            active,
            lax.dynamic_update_index_in_dim(padded_store, padded, slot_index, 0),
            padded_store,
        )
        received = shifted(outputs, "section", 1)
        return ((received, stored, padded_store, kept_conv), None)

    kept_start = jnp.zeros((1,), jnp.float32)
    padded_start = jnp.zeros((micro_count, positions + 2 * reach, channels), jnp.bfloat16)
    start_state = (zero_rows, jnp.zeros_like(inputs), padded_start, kept_start)
    (unused_rows, stored, padded_store, kept_conv), unused_out = lax.scan(
        forward_tick, start_state, all_ticks
    )

    def backward_tick(state_tuple, tick_index):
        received, carried, input_grads = state_tuple
        micro_step = tick_index - (section_count - 1 - section_index)
        active = (micro_step >= 0) & (micro_step < micro_count)
        slot_index = jnp.clip(micro_step, 0, micro_count - 1)
        own_rows = lax.dynamic_index_in_dim(grad_out, slot_index, 0, keepdims=False)
        upstream = jnp.where(section_index == section_count - 1, own_rows, received)
        saved_rows = lax.dynamic_index_in_dim(stored, slot_index, 0, keepdims=False)
        saved_pad = lax.dynamic_index_in_dim(padded_store, slot_index, 0, keepdims=False)

        def first_half():
            columns = tap_columns(saved_pad, dilation, reach, positions)
            conv_out = jnp.dot(columns, weight_conv, preferred_element_type=jnp.float32)
            mix_wide, pull_point = jax.vjp(norm_act, conv_out, scale_point)
            mixture = mix_wide.astype(jnp.bfloat16)
            grad_mixture = times_transposed(upstream, weight_point)
            grad_conv_wide, grad_sp = pull_point(grad_mixture)
            return (grad_conv_wide.astype(jnp.bfloat16), grad_sp, mixture, columns)

        def first_nothing():
            return (
                jnp.zeros((positions, inner), jnp.bfloat16),
                jnp.zeros((inner,), jnp.float32),
                jnp.zeros((positions, inner), jnp.bfloat16),
                jnp.zeros((positions, 3 * channels), jnp.bfloat16),
            )

        grad_conv, grad_sp, mixture, columns = lax.cond(active, first_half, first_nothing)
        grad_pad = with_halo(grad_conv, (("dp", 0),), reach)

        def second_half():
            ahead_rows = lax.dynamic_slice_in_dim(grad_pad, reach + dilation, positions, 0)
            behind = lax.dynamic_slice_in_dim(grad_pad, reach - dilation, positions, 0)
            grad_acts = times_transposed(ahead_rows, tap_weights[0]) + times_transposed(
                grad_conv, tap_weights[1]
            )
            grad_acts = grad_acts + times_transposed(behind, tap_weights[2])
            widened = saved_rows.astype(jnp.float32)
            unused_acts, pull_conv = jax.vjp(norm_act, widened, scale_conv)
            grad_widened, grad_sc = pull_conv(grad_acts)
            downstream = (upstream.astype(jnp.float32) + grad_widened).astype(jnp.bfloat16)
            gain_c, gain_p, first_acc, second_acc, third_acc = carried
            gain_c = gain_c + grad_sc
            gain_p = gain_p + grad_sp
            first_acc = first_acc + contract_rows(columns, grad_conv)
            second_acc = second_acc + contract_rows(mixture, upstream)
            return (downstream, (gain_c, gain_p, first_acc, second_acc, third_acc))

        def second_nothing():
            return (zero_rows, carried)

        downstream, carried = lax.cond(active, second_half, second_nothing)
        input_grads = jnp.where(
            active,
            lax.dynamic_update_index_in_dim(input_grads, downstream, slot_index, 0),
            input_grads,
        )
        received = shifted(downstream, "section", -1)
        return ((received, carried, input_grads), None)

    first_start = jnp.zeros((3 * channels, inner), jnp.float32)
    second_start = jnp.zeros((inner, channels), jnp.float32)
    third_start = jnp.zeros((1,), jnp.float32)
    carried_start = (
        jnp.zeros((channels,), jnp.float32),
        jnp.zeros((inner,), jnp.float32),
        first_start,
        second_start,
        third_start,
    )
    (unused_back, carried, input_grads), unused_ys = lax.scan(
        backward_tick, (zero_rows, carried_start, jnp.zeros_like(inputs)), all_ticks
    )
    gain_c, gain_p, first_acc, second_acc, third_acc = carried
    share_conv, share_point, share_gc, share_gp = (
        lax.psum_scatter(first_acc, "dp", scatter_dimension=0, tiled=True),
        lax.psum_scatter(second_acc, "dp", scatter_dimension=0, tiled=True),
        lax.psum_scatter(gain_c, "dp", scatter_dimension=0, tiled=True),
        lax.psum_scatter(gain_p, "dp", scatter_dimension=0, tiled=True),
    )
    return (
        (share_conv * norm_scale)[None],
        (share_point * norm_scale)[None],
        (share_gc * norm_scale)[None],
        (share_gp * norm_scale)[None],
        input_grads[None],
    )


def solution(mesh):
    return jax.shard_map(
        on_device,
        mesh=mesh,
        in_specs=(
            P(None, "dp", None),
            P(None, "dp", None),
            P("section", None, None),
            P("section", None, None),
            P("section", None),
            P("section", None),
        ),
        out_specs=(
            P("section", "dp", None),
            P("section", "dp", None),
            P("section", "dp"),
            P("section", "dp"),
            P("section", None, "dp", None),
        ),
        check_vma=False,
    )
```

profile of v0, /device:TPU:32, one launch (start us, length us, event | category | flops | bytes accessed | tf_op | source)
XLA Modules:
  0.0 1277.1 jit_solution(12619214147741594773)
XLA Ops:
  9.5 222.9 %while.37 = (s32[]{:T(128)}, bf16[128,1536]{1,0:T(8,128)(2,1)S(1)}, bf16[2,128,1536]{2,1,0:T(8,128)(2,1)}, bf16[2,162,1536]{2,1,0:T(8,128)(2,1)S(1)}, s32[9]{0:T...) while((s32[]{:T(128)}, bf16[128,1536]{1,0:T(8,128)(2,1)S(1)}, ...), condition=%wide.region_5.6_spmd, body=%wide.region_0.5_spmd.sunk | while | flops 1218450688 | bytes 22839372 | solution.py:115
  23.7 9.0 conditional.6
  47.9 9.0 conditional.6
  72.1 13.1 %collective-permute-start.2 = (bf16[128,1536]{1,0:T(8,128)(2,1)S(1)}, bf16[128,1536]{1,0:T(8,128)(2,1)S(1)}, u32[]{:S(2)}, u32[]{:S(2)}) collective-permute-start(bf16[128,1536]{1,0:T(8,128)(2,1)S(1)} %get-tuple-element.968), channel_id=1, source_target_pairs={{0,32},{32,64},{64,96},{96,128},{128,160},{160,192},{192,224},{1,3... | collective-permute-start | bytes 1179656 | tf_op jit(solution)/shard_map/while/body/eval_jaxpr/ppermute | solution.py:31
  99.0 7.8 collective-permute-start.2
  121.3 16.7 %collective-permute-start.2 = (bf16[128,1536]{1,0:T(8,128)(2,1)S(1)}, bf16[128,1536]{1,0:T(8,128)(2,1)S(1)}, u32[]{:S(2)}, u32[]{:S(2)}) collective-permute-start(bf16[128,1536]{1,0:T(8,128)(2,1)S(1)} %get-tuple-element.968), channel_id=1, source_target_pairs={{0,32},{32,64},{64,96},{96,128},{128,160},{160,192},{192,224},{1,3... | collective-permute-start | bytes 1179656 | tf_op jit(solution)/shard_map/while/body/eval_jaxpr/ppermute | solution.py:31
  153.0 7.8 collective-permute-start.2
  175.7 7.8 collective-permute-start.2
  198.5 7.8 collective-permute-start.2
  221.2 9.9 collective-permute-start.2
  232.4 6.0 broadcast_in_dim.69
  242.1 543.2 %while.38 = (s32[]{:T(128)}, bf16[128,1536]{1,0:T(8,128)(2,1)S(1)}, f32[1536]{0:T(1024)S(1)}, f32[768]{0:T(1024)S(1)}, f32[4608,768]{1,0:T(8,128)}, /*index=5*/f...) while((s32[]{:T(128)}, bf16[128,1536]{1,0:T(8,128)(2,1)S(1)}, ...), condition=%wide.region_17.18_spmd, body=%wide.region_6.17_spmd.sunk | while | flops 3343772160 | bytes 124958904 | solution.py:189
  257.6 6.1 collective-permute-done.5
  279.0 7.0 collective-permute-done.5
  301.2 6.1 collective-permute-done.5
  322.5 9.1 collective-permute-done.5
  346.6 6.1 collective-permute-done.5
  357.1 5.8 collective-permute-start.4
  368.6 6.7 collective-permute-done.5
  379.7 6.4 collective-permute-start.4
  391.7 275.4 %collective-permute-done.5 = bf16[128,1536]{1,0:T(8,128)(2,1)S(1)} collective-permute-done((bf16[128,1536]{1,0:T(8,128)(2,1)S(1)}, bf16[128,1536]{1,0:T(8,128)(2,1)S(1)}, u32[]{:S(2)}, u32[]{:S(2)}) %collective-permute-start.5) | collective-permute-done | bytes 393248 | tf_op jit(solution)/shard_map/while/body/eval_jaxpr/ppermute | solution.py:31
  669.4 10.6 conditional.7
  681.9 6.1 collective-permute-start.4
  689.7 30.4 %conditional.8 = (bf16[128,1536]{1,0:T(8,128)(2,1)S(1)}, f32[1536]{0:T(1024)S(1)}, f32[768]{0:T(1024)S(1)}, f32[4608,768]{1,0:T(8,128)}, f32[768,1536]{1,0:T(8,128)}, /*index=5*/bf16[1,128,1536]{2,1,0:T(8,128)(2,1)}) conditional(s32[]{:T(128)} %convert_element_type.69, (f32[1536]{0:T(1024)S(1)}, f32[768]{0:T(1024)S(1)}, f32[4608,768]{1,0:T(8,128)}, ...), branch_computations={%region_12.12_spmd, %region_13.16_spmd} | conditional | flops 2126710272 | bytes 91882296 | solution.py:170
  704.7 12.3 convolution_add_fusion.1
  730.6 10.6 conditional.7
  743.1 6.5 collective-permute-start.4
  751.3 30.4 %conditional.8 = (bf16[128,1536]{1,0:T(8,128)(2,1)S(1)}, f32[1536]{0:T(1024)S(1)}, f32[768]{0:T(1024)S(1)}, f32[4608,768]{1,0:T(8,128)}, f32[768,1536]{1,0:T(8,128)}, /*index=5*/bf16[1,128,1536]{2,1,0:T(8,128)(2,1)}) conditional(s32[]{:T(128)} %convert_element_type.69, (f32[1536]{0:T(1024)S(1)}, f32[768]{0:T(1024)S(1)}, f32[4608,768]{1,0:T(8,128)}, ...), branch_computations={%region_12.12_spmd, %region_13.16_spmd} | conditional | flops 2126710272 | bytes 91882296 | solution.py:170
  766.3 12.3 convolution_add_fusion.1
  788.0 152.6 %all-reduce.2 = (f32[1536]{0:T(1024)S(1)}, f32[768]{0:T(1024)S(1)}) all-reduce(f32[1536]{0:T(1024)S(1)} %get-tuple-element.507, f32[768]{0:T(1024)S(1)} %get-tuple-element.508), channel_id=4, replica_groups=mesh['section'=8,'dp'=32] {'dp'}, use_global_device_ids=true, to_apply=%region_20.21.clone | all-reduce | flops 2304 | bytes 18432
  941.7 83.1 %reduce-scatter.5.cloned.1.call-done = f32[24,1536]{1,0:T(8,128)} async-done(((f32[768,1536]{1,0:T(8,128)}), f32[24,1536]{1,0:T(8,128)}) %reduce-scatter.5.cloned.1.call-update) | async-done | bytes 147472 | tf_op jit(solution)/shard_map/reduce_scatter | solution.py:195
  1026.5 242.0 %reduce-scatter.3.cloned.1.call-done = f32[144,768]{1,0:T(8,128)} async-done(((f32[4608,768]{1,0:T(8,128)}), f32[144,768]{1,0:T(8,128)}) %reduce-scatter.3.cloned.1.call-update) | async-done | bytes 442384 | tf_op jit(solution)/shard_map/reduce_scatter | solution.py:194
  (450 shorter events, 320.5 us)
Async XLA Ops:
  7.2 1017.7 %reduce-scatter.5.cloned.1.call-start = ((), (), s32[]{:S(2)}) async-start(), calls=%async_computation.3 | async-start | bytes 4866048 | tf_op jit(solution)/shard_map/reduce_scatter | solution.py:195
  72.1 14.4 %collective-permute-start.2 = (bf16[128,1536]{1,0:T(8,128)(2,1)S(1)}, bf16[128,1536]{1,0:T(8,128)(2,1)S(1)}, u32[]{:S(2)}, u32[]{:S(2)}) collective-permute-start(bf16[128,1536]{1,0:T(8,128)(2,1)S(1)} %get-tuple-element.968), channel_id=1, source_target_pairs={{0,32},{32,64},{64,96},{96,128},{128,160},{160,192},{192,224},{1,3... | collective-permute-start | bytes 1179656 | tf_op jit(solution)/shard_map/while/body/eval_jaxpr/ppermute | solution.py:31
  99.0 9.1 collective-permute-start.2
  121.3 18.0 %collective-permute-start.2 = (bf16[128,1536]{1,0:T(8,128)(2,1)S(1)}, bf16[128,1536]{1,0:T(8,128)(2,1)S(1)}, u32[]{:S(2)}, u32[]{:S(2)}) collective-permute-start(bf16[128,1536]{1,0:T(8,128)(2,1)S(1)} %get-tuple-element.968), channel_id=1, source_target_pairs={{0,32},{32,64},{64,96},{96,128},{128,160},{160,192},{192,224},{1,3... | collective-permute-start | bytes 1179656 | tf_op jit(solution)/shard_map/while/body/eval_jaxpr/ppermute | solution.py:31
  143.3 7.8 collective-permute-start
  145.2 7.5 collective-permute-start.1
  153.0 9.1 collective-permute-start.2
  166.0 7.8 collective-permute-start
  168.0 7.5 collective-permute-start.1
  175.7 9.1 collective-permute-start.2
  188.8 7.8 collective-permute-start
  190.7 7.5 collective-permute-start.1
  198.5 9.1 collective-permute-start.2
  211.5 7.8 collective-permute-start
  213.4 7.5 collective-permute-start.1
  221.2 11.2 collective-permute-start.2
  254.4 9.3 collective-permute-start.5
  275.8 10.1 collective-permute-start.5
  298.1 9.3 collective-permute-start.5
  319.4 12.2 collective-permute-start.5
  343.4 9.3 collective-permute-start.5
  355.2 7.8 collective-permute-start.3
  365.4 9.8 collective-permute-start.5
  377.7 8.3 collective-permute-start.3
  379.7 8.0 collective-permute-start.4
  388.6 278.5 %collective-permute-start.5 = (bf16[128,1536]{1,0:T(8,128)(2,1)S(1)}, bf16[128,1536]{1,0:T(8,128)(2,1)S(1)}, u32[]{:S(2)}, u32[]{:S(2)}) collective-permute-start(bf16[128,1536]{1,0:T(8,128)(2,1)S(1)} %get-tuple-element.825), channel_id=1, source_target_pairs={{32,0},{64,32},{96,64},{128,96},{160,128},{192,160},{224,192},{33,... | collective-permute-start | bytes 1179656 | tf_op jit(solution)/shard_map/while/body/eval_jaxpr/ppermute | solution.py:31
  680.0 8.0 collective-permute-start.3
  681.9 7.7 collective-permute-start.4
  720.1 8.2 collective-permute-start.5
  741.2 8.4 collective-permute-start.3
  743.1 8.1 collective-permute-start.4
  785.4 483.1 %reduce-scatter.3.cloned.1.call-start = ((), (), s32[]{:S(2)}) async-start(), calls=%async_computation.2 | async-start | bytes 14598144 | tf_op jit(solution)/shard_map/reduce_scatter | solution.py:194
  (70 other events, 472.9 us)
Sparse Core Ops, SparseCore 0:
  785.5 239.3 reduce-scatter.4
  1029.1 239.3 reduce-scatter.2
where the time goes:
time: 1280 us
  waiting for transfers between devices  694 us (54%)
  starting transfers between devices  213 us (17%)
  blocking collectives  153 us (12%)
  matrix products  73.1 us (6%)
  other arithmetic  63.9 us (5%)
  local copies, waits for them, and re-layouts  37 us (3%)
  loops' own time  28.1 us (2%)
  between operations  15.4 us (1%)
    ppermute x18, waiting for transfers between devices, shifted(): return lax.ppermute(shard, axis, pairs)  334 us
    reduce_scatter x1, waiting for transfers between devices, on_device(): lax.psum_scatter(first_acc, 'dp', scatter_dimension=0, tiled=True)  242 us
    unnamed x1, blocking collectives  153 us
    ppermute x18, starting transfers between devices, with_halo(): lax.ppermute(tail, axis, [(i, (i + 1) % count) for i in range(ends)])  91.2 us
    ppermute x18, starting transfers between devices, shifted(): return lax.ppermute(shard, axis, pairs)  85.2 us
    reduce_scatter x1, waiting for transfers between devices, on_device(): lax.psum_scatter(second_acc, 'dp', scatter_dimension=0, tiled=True)  83.1 us
    ppermute x18, starting transfers between devices, with_halo(): lax.ppermute(head, axis, [((i + 1) % count, i) for i in range(ends)])  36.4 us
    ppermute x18, waiting for transfers between devices, with_halo(): lax.ppermute(tail, axis, [(i, (i + 1) % count) for i in range(ends)])  31.7 us
  transfers between devices with their start and end apart: 56, of which 47 were waited for; matrix products, arithmetic and copies ran while one was open for 2% of the time, Pallas kernels for 0%

commit v1 on v0

v1 whole, which is shorter than its diff:
```python
import math

import jax
import jax.numpy as jnp
from jax import lax
from jax.sharding import PartitionSpec as P

EPSILON = 1e-06
Y_CHIPS = 4
GELU_SCALE = math.sqrt(2.0 / math.pi)
GELU_CUBIC = 0.044715


def normed(values):
    inverse = lax.rsqrt(jnp.mean(values * values, axis=-1, keepdims=True) + EPSILON)
    return values * inverse, inverse


def gelu_and_slope(u):
    tanh = jnp.tanh(GELU_SCALE * (u + GELU_CUBIC * u * u * u))
    half = 0.5 * (1.0 + tanh)
    slope = half + 0.5 * u * (1.0 - tanh * tanh) * GELU_SCALE * (1.0 + 3.0 * GELU_CUBIC * u * u)
    return u * half, slope


def act(values, gain):
    hat, unused = normed(values)
    return gelu_and_slope(hat * gain)[0]


def matmul(left, right):
    return lax.dot_general(
        left, right, (((left.ndim - 1,), (0,)), ((), ())), preferred_element_type=jnp.float32
    )


def matmul_t(left, right):
    return lax.dot_general(
        left, right, (((left.ndim - 1,), (1,)), ((), ())), preferred_element_type=jnp.float32
    )


def halo(rows, width, dp):
    left = lax.ppermute(rows[:, -width:], "dp", [(i, i + 1) for i in range(dp - 1)])
    right = lax.ppermute(rows[:, :width], "dp", [(i + 1, i) for i in range(dp - 1)])
    return left, right


def on_device(inputs, grad_out, w_conv, w_point, gain_conv, gain_point):
    micro, positions, channels = inputs.shape
    section = lax.axis_index("section")
    sections = lax.axis_size("section")
    dp_index = lax.axis_index("dp")
    dp = lax.axis_size("dp")
    ny = Y_CHIPS
    nz = dp // ny
    y_groups = [[y * nz + z for y in range(ny)] for z in range(nz)]
    z_groups = [[y * nz + z for z in range(nz)] for y in range(ny)]
    length = positions * dp
    norm_scale = 1.0 / math.sqrt(micro * length)
    dil = [3**s // 2**s for s in range(sections)]
    reach = dil[-1]
    ahead = [sum(dil[s : sections - 1]) for s in range(sections)]
    back = [sum(dil[:s]) for s in range(sections + 1)]
    wide = back[sections]
    outer = wide + reach
    dilation = jnp.array(dil, jnp.int32)[section]
    inner = w_conv.shape[2]
    weight_conv = w_conv[0]
    taps = weight_conv.reshape(3, channels, inner)
    weight_point = w_point[0]
    g_conv = gain_conv[0][None]
    g_point = gain_point[0][None]

    def inside(ext):
        place = lax.broadcasted_iota(jnp.int32, (positions + 2 * ext, 1), 0) + (
            dp_index * positions - ext
        )
        return (place >= 0) & (place < length)

    def hop(rows, source, target):
        pairs = [(source * dp + i, target * dp + i) for i in range(dp)]
        return lax.ppermute(rows, ("section", "dp"), pairs)

    left, right = halo(inputs, ahead[0], dp)
    current = [jnp.concatenate([left[m], inputs[m], right[m]], axis=0) for m in range(micro)]
    kept = [inputs[m] for m in range(micro)]
    for s in range(sections - 1):
        rows = positions + 2 * ahead[s + 1]
        d = dil[s]
        for m in range(micro):
            wide_x = current[m].astype(jnp.float32)
            a = act(wide_x, g_conv).astype(jnp.bfloat16)
            conv = matmul(a[:rows], taps[0])
            conv = conv + matmul(a[d : d + rows], taps[1])
            conv = conv + matmul(a[2 * d : 2 * d + rows], taps[2])
            b = act(conv, g_point).astype(jnp.bfloat16)
            out = (wide_x[d : d + rows] + matmul(b, weight_point)).astype(jnp.bfloat16)
            out = jnp.where(inside(ahead[s + 1]), out, jnp.zeros_like(out))
            current[m] = hop(out, s, s + 1)
            mine = current[m][ahead[s + 1] : ahead[s + 1] + positions]
            kept[m] = jnp.where(section == s + 1, mine, kept[m])

    x_main = jnp.stack(kept)
    left, right = halo(x_main, outer, dp)
    x_ext = jnp.concatenate([left, x_main, right], axis=1)
    x_wide = x_ext.astype(jnp.float32)
    x_hat, x_inv = normed(x_wide)
    a_wide, x_slope = gelu_and_slope(x_hat * g_conv)
    a_ext = a_wide.astype(jnp.bfloat16)
    conv_rows = positions + 2 * wide

    def tap_rows(array, start, count, dim):
        return [
            lax.dynamic_slice_in_dim(array, start + (k - 1) * dilation, count, dim)
            for k in range(3)
        ]

    columns = tap_rows(a_ext, outer - wide, conv_rows, 1)
    conv = sum(matmul(columns[k], taps[k]) for k in range(3))
    v_hat, v_inv = normed(conv)
    b_wide, v_slope = gelu_and_slope(v_hat * g_point)
    b_main = b_wide[:, wide : wide + positions].astype(jnp.bfloat16)
    core = slice(outer - back[sections - 1], outer + positions + back[sections - 1])
    x_res = lax.optimization_barrier((x_hat[:, core], x_inv[:, core], x_slope[:, core]))
    v_res = lax.optimization_barrier((v_hat, v_inv, v_slope))
    x_hat, x_inv, x_slope = x_res
    v_hat, v_inv, v_slope = v_res

    a_send = a_ext[:, outer - reach : outer + positions + reach]
    a_all = lax.all_gather(a_send, "dp", axis=0, axis_index_groups=y_groups)
    b_all = lax.all_gather(b_main, "dp", axis=0, axis_index_groups=y_groups)
    count = ny * micro * positions
    a_cols = tap_rows(a_all, reach, positions, 2)
    a_cols = jnp.concatenate([c.reshape(count, channels) for c in a_cols], axis=1)
    b_cols = b_all.reshape(count, inner)

    def act_pull(grad, gain, hat, inverse, slope):
        w = grad * slope * gain
        return inverse * (w - hat * jnp.mean(w * hat, axis=-1, keepdims=True))

    left, right = halo(grad_out, wide, dp)
    current = [jnp.concatenate([left[m], grad_out[m], right[m]], axis=0) for m in range(micro)]
    zero_q = jnp.zeros((positions + 2 * reach, inner), jnp.bfloat16)
    kept_in = [grad_out[m] for m in range(micro)]
    kept_q = [zero_q for m in range(micro)]
    kept_out = [grad_out[m] for m in range(micro)]
    for s in reversed(range(sections)):
        rows = positions + 2 * back[s]
        d = dil[s]
        here = section == s
        for m in range(micro):
            e = current[m]
            part = slice(wide - back[s + 1], wide + positions + back[s + 1])
            grad_b = matmul_t(e, weight_point)
            q = act_pull(grad_b, g_point, v_hat[m, part], v_inv[m, part], v_slope[m, part])
            q = q.astype(jnp.bfloat16)
            r = matmul_t(q[2 * d : 2 * d + rows], taps[0])
            r = r + matmul_t(q[d : d + rows], taps[1])
            r = r + matmul_t(q[:rows], taps[2])
            base = back[sections - 1]
            part = slice(base - back[s], base + positions + back[s])
            t = act_pull(r, g_conv, x_hat[m, part], x_inv[m, part], x_slope[m, part])
            out = (e[d : d + rows].astype(jnp.float32) + t).astype(jnp.bfloat16)
            out = jnp.where(inside(back[s]), out, jnp.zeros_like(out))
            if s > 0:
                current[m] = hop(out, s, s - 1)
            ext = back[s + 1]
            if ext >= reach:
                mine_q = q[ext - reach : ext + positions + reach]
            else:
                mine_q = jnp.pad(q, ((reach - ext, reach - ext), (0, 0)))
            kept_q[m] = jnp.where(here, mine_q, kept_q[m])
            kept_in[m] = jnp.where(here, e[ext : ext + positions], kept_in[m])
            kept_out[m] = jnp.where(here, out[back[s] : back[s] + positions], kept_out[m])

    q_keep = jnp.stack(kept_q)
    e_keep = jnp.stack(kept_in)
    grad_acts = jnp.stack(kept_out)
    q_main = q_keep[:, reach : reach + positions].reshape(micro * positions, inner)
    e_main = e_keep.reshape(micro * positions, channels)

    def column_blocks(array):
        blocks = array.reshape(array.shape[0], ny, array.shape[1] // ny)
        return blocks.transpose(1, 0, 2)

    def swap_y(array):
        return lax.all_to_all(array, "dp", 0, 0, axis_index_groups=y_groups)

    q_part = inner // ny
    send = jnp.concatenate([column_blocks(q_main), column_blocks(e_main)], axis=2)
    got = swap_y(send).reshape(count, q_part + channels // ny)
    q_got, e_got = got[:, :q_part], got[:, q_part:]

    def contract(left, right):
        return lax.dot_general(
            left, right, (((0,), (0,)), ((), ())), preferred_element_type=jnp.float32
        )

    grad_conv = contract(a_cols, q_got).astype(jnp.bfloat16)
    grad_point = contract(b_cols, e_got).astype(jnp.bfloat16)
    conv_own = 3 * channels // dp
    point_own = inner // dp
    half = conv_own // 2
    conv_pack = grad_conv.reshape(ny, nz, 2, half, q_part)
    pack = jnp.concatenate(
        [
            jnp.concatenate([conv_pack[:, :, 0], conv_pack[:, :, 1]], axis=-1),
            grad_point.reshape(ny, nz, point_own, channels // ny),
        ],
        axis=2,
    )
    pack = pack.transpose(1, 0, 2, 3).reshape(nz * ny * (half + point_own), 2 * q_part)
    total = lax.psum_scatter(
        pack, "dp", scatter_dimension=0, axis_index_groups=z_groups, tiled=True
    ).reshape(ny, half + point_own, 2 * q_part)

    q_late, e_late, unused = lax.optimization_barrier((q_keep, e_keep, pack))
    mid = slice(wide, wide + positions)
    grad_b = matmul_t(e_late, weight_point)
    gain_p = jnp.sum(grad_b * v_slope[:, mid] * v_hat[:, mid], axis=(0, 1))
    q_cols = tap_rows(q_late, reach, positions, 1)
    r = sum(matmul_t(q_cols[2 - k], taps[k]) for k in range(3))
    mid = slice(back[sections - 1], back[sections - 1] + positions)
    gain_c = jnp.sum(r * x_slope[:, mid] * x_hat[:, mid], axis=(0, 1))
    gains = jnp.concatenate(
        [gain_c.reshape(dp, channels // dp), gain_p.reshape(dp, inner // dp)], axis=1
    )
    gains = gains.reshape(ny, nz, -1).transpose(1, 0, 2)
    gains = lax.all_to_all(gains, "dp", 0, 0, axis_index_groups=z_groups).sum(0)
    gains = swap_y(gains).sum(0) * norm_scale

    own = swap_y(total).astype(jnp.float32) * norm_scale
    own_conv = own[:, :half].reshape(ny, half, 2, q_part)
    own_conv = own_conv.transpose(2, 1, 0, 3).reshape(conv_own, inner)
    own_point = own[:, half:].transpose(1, 0, 2).reshape(point_own, channels)
    return (
        own_conv[None],
        own_point[None],
        gains[: channels // dp][None],
        gains[channels // dp :][None],
        grad_acts[None],
    )


def solution(mesh):
    return jax.shard_map(
        on_device,
        mesh=mesh,
        in_specs=(
            P(None, "dp", None),
            P(None, "dp", None),
            P("section", None, None),
            P("section", None, None),
            P("section", None),
            P("section", None),
        ),
        out_specs=(
            P("section", "dp", None),
            P("section", "dp", None),
            P("section", "dp"),
            P("section", "dp"),
            P("section", None, "dp", None),
        ),
        check_vma=False,
    )
```

time: 1280 us -> 481 us (0.38)
  waiting for transfers between devices: 694 us -> 87 us
  blocking collectives: 153 us -> 0 us
  starting transfers between devices: 213 us -> 67.5 us
  matrix products: 73.1 us -> 161 us
  loops' own time: 28.1 us -> 0 us
  local copies, waits for them, and re-layouts: 37 us -> 58 us
  other arithmetic: 63.9 us -> 78.3 us
    reduce_scatter x2 -> x1, waiting for transfers between devices: 325 us -> 0.01 us  [on_device(): lax.psum_scatter(pack, 'dp', scatter_dimension=0, axis_index_groups=z_gro...]
    ppermute x54 -> x34, waiting for transfers between devices: 368 us -> 67.2 us  [the longest x28 59.7 us: hop(): return lax.ppermute(rows, ('section', 'dp'), pairs)]
    ppermute x54 -> x34, starting transfers between devices: 213 us -> 48.7 us  [the longest x28 29.7 us: hop(): return lax.ppermute(rows, ('section', 'dp'), pairs)]
    unnamed x1 -> x0, blocking collectives: 153 us -> none
    dot_general x18 -> x129, matrix products: 73.1 us -> 161 us  [the longest x68 95.7 us: matmul_t(): lax.dot_general(left, right, (((left.ndim - 1,), (1,)), ((), ())), prefer...]
    select_n x36 -> x7, other arithmetic: 47.1 us -> 12.1 us  [on_device(): out = jnp.where(inside(back[s]), out, jnp.zeros_like(out))]
    another operation x29 -> x0, loops' own time: 28.1 us -> none  [the longest x1 6.81 us: on_device(): lax.scan(backward_tick, (zero_rows, carried_start, jnp.zeros_like(inputs)...]
    another operation x15 -> x13, other arithmetic: 0.32 us -> 21.3 us  [the longest x2 8.34 us: on_device(): grad_acts = jnp.stack(kept_out)]
  transfers between devices with their start and end apart: 56 -> 41, of which waited for: 47 -> 8; matrix products, arithmetic and copies ran while one was open for 2% -> 42% of each run, Pallas kernels for 0% -> 0%
where the time goes in v1:
time: 481 us; the launch traced here: 472 us
  matrix products  161 us (33%)
  waiting for transfers between devices  87 us (18%)
  other arithmetic  78.3 us (16%)
  starting transfers between devices  67.5 us (14%)
  local copies, waits for them, and re-layouts  58 us (12%)
  between operations  20.1 us (4%)
    dot_general x68, matrix products, matmul_t(): lax.dot_general(left, right, (((left.ndim - 1,), (1,)), ((), ())), prefer...  95.7 us
    ppermute x28, waiting for transfers between devices, hop(): return lax.ppermute(rows, ('section', 'dp'), pairs)  59.7 us
    dot_general x59, matrix products, matmul(): lax.dot_general(left, right, (((left.ndim - 1,), (0,)), ((), ())), prefer...  53.1 us
    ppermute x28, starting transfers between devices, hop(): return lax.ppermute(rows, ('section', 'dp'), pairs)  29.7 us
    all_to_all x3, waiting for transfers between devices, swap_y(): return lax.all_to_all(array, 'dp', 0, 0, axis_index_groups=y_groups)  17.9 us
    select_n x7, other arithmetic, on_device(): out = jnp.where(inside(back[s]), out, jnp.zeros_like(out))  12.1 us
    dot_general x2, matrix products, contract(): lax.dot_general(left, right, (((0,), (0,)), ((), ())), preferred_element_...  11.9 us
    all_to_all x3, starting transfers between devices, swap_y(): return lax.all_to_all(array, 'dp', 0, 0, axis_index_groups=y_groups)  11.1 us
  transfers between devices with their start and end apart: 41, of which 8 were waited for; matrix products, arithmetic and copies ran while one was open for 42% of the time, Pallas kernels for 0%

profile of v1, /device:TPU:32, one launch (start us, length us, event | category | flops | bytes accessed | tf_op | source)
XLA Modules:
  0.0 471.6 jit_solution(17074104648271409143)
XLA Ops:
  9.3 3.9 collective-permute-start
  13.2 2.7 collective-permute-start.1
  17.8 3.2 collective-permute-start.18
  21.0 3.4 collective-permute-start.19
  133.1 3.5 collective-permute-start.16
  140.0 2.8 collective-permute-done.16
  142.8 4.7 collective-permute-done.17
  147.9 2.7 broadcast_multiply_fusion
  197.4 2.7 fusion.236
  228.1 2.7 fusion.232
  237.2 3.0 fusion.833
  262.7 59.0 %collective-permute-done.26 = bf16[130,1536]{1,0:T(8,128)(2,1)S(1)} collective-permute-done((bf16[130,1536]{1,0:T(8,128)(2,1)S(1)}, bf16[130,1536]{1,0:T(8,128)(2,1)S(1)}, u32[]{:S(2)}, u32[]{:S(2)}) %collective-permute-start.26) | collective-permute-done | bytes 399392 | tf_op jit(solution)/shard_map/ppermute | solution.py:83
  331.3 2.9 fusion.910
  344.2 4.5 all-to-all-start
  348.9 2.6 fusion.244
  351.5 3.5 convolution_add_fusion.35
  360.1 3.7 fusion.45
  363.8 8.4 %all-to-all-done = bf16[4,256,576]{1,2,0:T(8,128)(2,1)} async-done(((bf16[4,256,576]{1,2,0:T(8,128)(2,1)}), bf16[4,256,576]{1,2,0:T(8,128)(2,1)}, u32[]{:S(2)}, u32[]{:S(2)}) %all-to-all-start) | async-done | bytes 1179680 | tf_op jit(solution)/shard_map/all_to_all | solution.py:188
  374.7 3.5 convolution_convert_fusion
  378.2 10.9 %constant_dynamic-slice_fusion.1 = (bf16[4,2,128,1536]{3,2,1,0:T(8,128)(2,1)S(1)}, bf16[4,2,128,1536]{3,2,1,0:T(8,128)(2,1)S(1)}, bf16[4,2,128,1536]{3,2,1,0:T(8,128)(2,1)}) fusion(bf16[4,2,162,1536]{3,2,1,0:T(8,128)(2,1)} %bitcast.1121, s32[]{:T(128)S(6)} %select_n.437, s32[]{:T(128)S(6)} %select_n.438), kind=kLoop, calls=%fused_computation.1192 | loop fusion | bytes 18874376 | tf_op jit(solution)/shard_map/dynamic_slice | solution.py:115
  389.0 8.4 %fusion.6 = bf16[4608,192]{0,1:T(8,128)(2,1)} fusion(bf16[1024,1536]{1,0:T(8,128)(2,1)S(1)} %bitcast.1125, bf16[1024,1536]{1,0:T(8,128)(2,1)} %bitcast.1126, bf16[1024,1536]{1,0:T(8,128)(2,1)S(1)} %bitcast.1124, bf16[1024,576]{0,1:T(8,128)(2,1)} %bitcast.1131), kind=kOutput, calls=%fused_computation.6 | convolution fusion | flops 1841135616 | bytes 11599872 | tf_op jit(solution)/shard_map/dot_general | solution.py:196
  397.5 4.0 copy.38
  405.9 4.9 %fusion.651 = (f32[128]{0:T(128)S(1)}, f32[128]{0:T(128)S(1)}, f32[128,1536]{1,0:T(8,128)}) fusion(f32[2,188,1536]{2,1,0:T(8,128)} %copy-done.2, f32[128,1536]{1,0:T(8,128)} %fusion.45, f32[1536]{0:T(1024)S(1)} %reduce.1, f32[2,188,1536]{2,1,0:T(8,128)} %copy-done.11, f32[128,1536]{1,0:T(8,128)} %convolution_add_fusion.35, ...), kind=kOutput, calls=%fused_computation.657 | convolution fusion | flops 303365888 | bytes 7281664 | tf_op jit(solution)/shard_map/dot_general | solution.py:38
  411.4 3.4 fusion.880
  414.9 2.7 fusion.64
  421.0 3.1 fusion.463
  426.3 7.5 %all-to-all-start.2 = ((f32[8,4,72]{2,1,0:T(4,128)}), f32[8,4,72]{2,1,0:T(4,128)S(1)}, u32[]{:S(2)}, u32[]{:S(2)}) async-start(f32[8,4,72]{2,1,0:T(4,128)} %copy.42), calls=%async_computation.3 | async-start | bytes 32768 | tf_op jit(solution)/shard_map/all_to_all | solution.py:230
  433.7 4.9 %fusion.877 = bf16[1,128,1536]{2,1,0:T(8,128)(2,1)} fusion(f32[128,1536]{1,0:T(8,128)} %get-tuple-element.206, f32[2,188,1536]{2,1,0:T(8,128)} %copy-done.2, bf16[188,1536]{1,0:T(8,128)(2,1)} %copy-done.74, bf16[166,1536]{1,0:T(8,128)(2,1)} %copy-done.77, bf16[152,1536]{1,0:T(8,128)(2,1)} %get-tuple-element.67, bf16[142,1536]{1,0:T(8,128)(2,1)} %copy-done.80, ...), kind=kLoop, calls=%fused_computation.941 | loop fusion | flops 2949120 | bytes 5506184 | tf_op jit(solution)/shard_map/stack | solution.py:179
  441.0 3.2 all-to-all-start.3
  446.2 3.2 all-to-all-done.3
  450.0 3.5 all-to-all-start.1
  454.0 6.3 %all-to-all-done.1 = bf16[4,96,384]{2,1,0:T(8,128)(2,1)S(1)} async-done(((bf16[4,96,384]{2,1,0:T(8,128)(2,1)}), bf16[4,96,384]{2,1,0:T(8,128)(2,1)S(1)}, u32[]{:S(2)}, u32[]{:S(2)}) %all-to-all-start.1) | async-done | bytes 294944 | tf_op jit(solution)/shard_map/all_to_all | solution.py:188
  (630 shorter events, 262.4 us)
Async XLA Ops:
  7.2 367.5 %all-gather.7.cloned.1.call-start = ((), (), s32[]{:S(2)}) async-start(), calls=%async_computation.7 | async-start | bytes 1966080 | tf_op jit(solution)/shard_map/all_gather | solution.py:132
  9.3 18.2 %collective-permute-start = (bf16[2,30,1536]{2,1,0:T(8,128)(2,1)}, bf16[2,30,1536]{2,1,0:T(8,128)(2,1)}, u32[]{:S(2)}, u32[]{:S(2)}) collective-permute-start(bf16[2,30,1536]{2,1,0:T(8,128)(2,1)} %get-tuple-element.103), channel_id=1, source_target_pairs={{0,1},{1,2},{2,3},{3,4},{4,5},{5,6},{6,7},{7,8},{8,9},{9,10},{10,1... | collective-permute-start | bytes 552968 | tf_op jit(solution)/shard_map/ppermute | solution.py:44
  13.2 15.2 %collective-permute-start.1 = (bf16[2,30,1536]{2,1,0:T(8,128)(2,1)}, bf16[2,30,1536]{2,1,0:T(8,128)(2,1)}, u32[]{:S(2)}, u32[]{:S(2)}) collective-permute-start(bf16[2,30,1536]{2,1,0:T(8,128)(2,1)} %get-tuple-element.104), channel_id=1, source_target_pairs={{1,0},{2,1},{3,2},{4,3},{5,4},{6,5},{7,6},{8,7},{9,8},{10,9},{11,1... | collective-permute-start | bytes 552968 | tf_op jit(solution)/shard_map/ppermute | solution.py:45
  17.8 102.4 %collective-permute-start.18 = (bf16[2,47,1536]{2,1,0:T(8,128)(2,1)}, bf16[2,47,1536]{2,1,0:T(8,128)(2,1)}, u32[]{:S(2)}, u32[]{:S(2)}) collective-permute-start(bf16[2,47,1536]{2,1,0:T(8,128)(2,1)} %get-tuple-element.97), channel_id=1, source_target_pairs={{0,1},{1,2},{2,3},{3,4},{4,5},{5,6},{6,7},{7,8},{8,9},{9,10},{10,1... | collective-permute-start | bytes 866312 | tf_op jit(solution)/shard_map/ppermute | solution.py:44
  21.0 117.9 %collective-permute-start.19 = (bf16[2,47,1536]{2,1,0:T(8,128)(2,1)}, bf16[2,47,1536]{2,1,0:T(8,128)(2,1)}, u32[]{:S(2)}, u32[]{:S(2)}) collective-permute-start(bf16[2,47,1536]{2,1,0:T(8,128)(2,1)} %get-tuple-element.98), channel_id=1, source_target_pairs={{1,0},{2,1},{3,2},{4,3},{5,4},{6,5},{7,6},{8,7},{9,8},{10,9},{11,1... | collective-permute-start | bytes 866312 | tf_op jit(solution)/shard_map/ppermute | solution.py:45
  35.5 6.3 %collective-permute-start.9 = (bf16[186,1536]{1,0:T(8,128)(2,1)S(1)}, bf16[186,1536]{1,0:T(8,128)(2,1)S(1)}, u32[]{:S(2)}, u32[]{:S(2)}) collective-permute-start(bf16[186,1536]{1,0:T(8,128)(2,1)S(1)} %fusion.48), channel_id=1, source_target_pairs={{0,32},{1,33},{2,34},{3,35},{4,36},{5,37},{6,38},{7,39},{8,40},{9,... | collective-permute-start | bytes 1714184 | tf_op jit(solution)/shard_map/ppermute | solution.py:83
  39.7 2.9 collective-permute-start.2
  48.2 4.2 collective-permute-start.10
  58.2 4.7 %collective-permute-start.11 = (bf16[180,1536]{1,0:T(8,128)(2,1)S(1)}, bf16[180,1536]{1,0:T(8,128)(2,1)S(1)}, u32[]{:S(2)}, u32[]{:S(2)}) collective-permute-start(bf16[180,1536]{1,0:T(8,128)(2,1)S(1)} %fusion.729), channel_id=1, source_target_pairs={{64,96},{65,97},{66,98},{67,99},{68,100},{69,101},{70,102},{71,103... | collective-permute-start | bytes 1658888 | tf_op jit(solution)/shard_map/ppermute | solution.py:83
  69.3 6.5 %collective-permute-start.12 = (bf16[174,1536]{1,0:T(8,128)(2,1)}, bf16[174,1536]{1,0:T(8,128)(2,1)}, u32[]{:S(2)}, u32[]{:S(2)}) collective-permute-start(bf16[174,1536]{1,0:T(8,128)(2,1)} %fusion.755), channel_id=1, source_target_pairs={{96,128},{97,129},{98,130},{99,131},{100,132},{101,133},{102,134},... | collective-permute-start | bytes 1603592 | tf_op jit(solution)/shard_map/ppermute | solution.py:83
  73.2 3.8 collective-permute-start.5
  91.6 11.5 %collective-permute-start.13 = (bf16[164,1536]{1,0:T(8,128)(2,1)}, bf16[164,1536]{1,0:T(8,128)(2,1)}, u32[]{:S(2)}, u32[]{:S(2)}) collective-permute-start(bf16[164,1536]{1,0:T(8,128)(2,1)} %fusion.777), channel_id=1, source_target_pairs={{128,160},{129,161},{130,162},{131,163},{132,164},{133,165},{134,1... | collective-permute-start | bytes 1511432 | tf_op jit(solution)/shard_map/ppermute | solution.py:83
  96.6 7.9 %collective-permute-start.6 = (bf16[164,1536]{1,0:T(8,128)(2,1)}, bf16[164,1536]{1,0:T(8,128)(2,1)}, u32[]{:S(2)}, u32[]{:S(2)}) collective-permute-start(bf16[164,1536]{1,0:T(8,128)(2,1)} %fusion.776), channel_id=1, source_target_pairs={{128,160},{129,161},{130,162},{131,163},{132,164},{133,165},{134,1... | collective-permute-start | bytes 1511432 | tf_op jit(solution)/shard_map/ppermute | solution.py:83
  116.3 5.0 %collective-permute-start.14 = (bf16[150,1536]{1,0:T(8,128)(2,1)S(1)}, bf16[150,1536]{1,0:T(8,128)(2,1)S(1)}, u32[]{:S(2)}, u32[]{:S(2)}) collective-permute-start(bf16[150,1536]{1,0:T(8,128)(2,1)S(1)} %fusion.807), channel_id=1, source_target_pairs={{160,192},{161,193},{162,194},{163,195},{164,196},{165,197},{166,1... | collective-permute-start | bytes 1382408 | tf_op jit(solution)/shard_map/ppermute | solution.py:83
  124.8 3.9 collective-permute-start.15
  127.9 3.0 collective-permute-start.8
  133.1 9.7 %collective-permute-start.16 = (bf16[2,64,1536]{2,1,0:T(8,128)(2,1)S(1)}, bf16[2,64,1536]{2,1,0:T(8,128)(2,1)S(1)}, u32[]{:S(2)}, u32[]{:S(2)}) collective-permute-start(bf16[2,64,1536]{2,1,0:T(8,128)(2,1)S(1)} %get-tuple-element.99), channel_id=1, source_target_pairs={{0,1},{1,2},{2,3},{3,4},{4,5},{5,6},{6,7},{7,8},{8,9},{9,10},{10,1... | collective-permute-start | bytes 1179656 | tf_op jit(solution)/shard_map/ppermute | solution.py:44
  136.6 10.9 %collective-permute-start.17 = (bf16[2,64,1536]{2,1,0:T(8,128)(2,1)S(1)}, bf16[2,64,1536]{2,1,0:T(8,128)(2,1)S(1)}, u32[]{:S(2)}, u32[]{:S(2)}) collective-permute-start(bf16[2,64,1536]{2,1,0:T(8,128)(2,1)S(1)} %get-tuple-element.100), channel_id=1, source_target_pairs={{1,0},{2,1},{3,2},{4,3},{5,4},{6,5},{7,6},{8,7},{9,8},{10,9},{11,1... | collective-permute-start | bytes 1179656 | tf_op jit(solution)/shard_map/ppermute | solution.py:45
  190.4 3.3 collective-permute-start.29
  192.8 3.2 collective-permute-start.22
  220.1 3.1 collective-permute-start.31
  221.6 3.8 collective-permute-start.24
  223.1 155.1 %all-gather.5.cloned.1.call-start = ((), (), s32[]{:S(2)}) async-start(), calls=%async_computation.6 | async-start | bytes 5160960 | tf_op jit(solution)/shard_map/all_gather | solution.py:131
  240.2 3.7 collective-permute-start.32
  240.9 5.1 %collective-permute-start.25 = (bf16[132,1536]{1,0:T(8,128)(2,1)}, bf16[132,1536]{1,0:T(8,128)(2,1)}, u32[]{:S(2)}, u32[]{:S(2)}) collective-permute-start(bf16[132,1536]{1,0:T(8,128)(2,1)} %get-tuple-element.61), channel_id=1, source_target_pairs={{64,32},{65,33},{66,34},{67,35},{68,36},{69,37},{70,38},{71,39},{7... | collective-permute-start | bytes 1216520 | tf_op jit(solution)/shard_map/ppermute | solution.py:83
  259.5 62.3 %collective-permute-start.26 = (bf16[130,1536]{1,0:T(8,128)(2,1)S(1)}, bf16[130,1536]{1,0:T(8,128)(2,1)S(1)}, u32[]{:S(2)}, u32[]{:S(2)}) collective-permute-start(bf16[130,1536]{1,0:T(8,128)(2,1)S(1)} %get-tuple-element.59), channel_id=1, source_target_pairs={{32,0},{33,1},{34,2},{35,3},{36,4},{37,5},{38,6},{39,7},{40,8},{41... | collective-permute-start | bytes 1198088 | tf_op jit(solution)/shard_map/ppermute | solution.py:83
  260.8 62.6 %collective-permute-start.33 = (bf16[130,1536]{1,0:T(8,128)(2,1)S(1)}, bf16[130,1536]{1,0:T(8,128)(2,1)S(1)}, u32[]{:S(2)}, u32[]{:S(2)}) collective-permute-start(bf16[130,1536]{1,0:T(8,128)(2,1)S(1)} %get-tuple-element.60), channel_id=1, source_target_pairs={{32,0},{33,1},{34,2},{35,3},{36,4},{37,5},{38,6},{39,7},{40,8},{41... | collective-permute-start | bytes 1198088 | tf_op jit(solution)/shard_map/ppermute | solution.py:83
  344.2 28.1 %all-to-all-start = ((bf16[4,256,576]{1,2,0:T(8,128)(2,1)}), bf16[4,256,576]{1,2,0:T(8,128)(2,1)}, u32[]{:S(2)}, u32[]{:S(2)}) async-start(bf16[4,256,576]{1,2,0:T(8,128)(2,1)} %pad_maximum_fusion.1), calls=%async_computation | async-start | bytes 2359296 | tf_op jit(solution)/shard_map/all_to_all | solution.py:188
  348.6 101.4 %reduce-scatter.2.cloned.1.call-start = ((), (), s32[]{:S(2)}) async-start(), calls=%async_computation.5 | async-start | bytes 2654208 | tf_op jit(solution)/shard_map/reduce_scatter | solution.py:214
  426.3 14.2 %all-to-all-start.2 = ((f32[8,4,72]{2,1,0:T(4,128)}), f32[8,4,72]{2,1,0:T(4,128)S(1)}, u32[]{:S(2)}, u32[]{:S(2)}) async-start(f32[8,4,72]{2,1,0:T(4,128)} %copy.42), calls=%async_computation.3 | async-start | bytes 32768 | tf_op jit(solution)/shard_map/all_to_all | solution.py:230
  441.0 8.4 %all-to-all-start.3 = ((f32[4,1,72]{2,1,0:T(1,128)}), f32[4,1,72]{2,1,0:T(1,128)S(1)}, u32[]{:S(2)}, u32[]{:S(2)}) async-start(f32[4,1,72]{2,1,0:T(1,128)} %bitcast.140), calls=%async_computation.4 | async-start | bytes 4096 | tf_op jit(solution)/shard_map/all_to_all | solution.py:188
  450.0 10.3 %all-to-all-start.1 = ((bf16[4,96,384]{2,1,0:T(8,128)(2,1)}), bf16[4,96,384]{2,1,0:T(8,128)(2,1)S(1)}, u32[]{:S(2)}, u32[]{:S(2)}) async-start(bf16[4,96,384]{2,1,0:T(8,128)(2,1)} %bitcast.1133), calls=%async_computation.2 | async-start | bytes 589824 | tf_op jit(solution)/shard_map/all_to_all | solution.py:188
  (128 other events, 849.0 us)
Sparse Core Ops, SparseCore 0:
  223.2 84.1 all-gather.6
  309.2 56.4 all-gather.4
  405.9 41.2 reduce-scatter.1
